TPU v7x, 32 devices: a whole 2x2x4 slice. The times are simulated.
32 devices in a mesh: arc: 8 (over z, x), vec: 4 (over y, core).
Axes of the slice: x: 2, y: 2, z: 4, core: 2. Of those that a mesh axis runs over, the one named last changes fastest.
Arguments:
- right_side: float32 [640, 128, 128], P(('arc', 'vec')), may hold values from -6 to 6
- prior_diag: float32 [640, 128], P(('arc', 'vec')), may hold values from 0.5 to 4
- inv_factor: bfloat16 [512, 256, 256], P(('arc', 'vec'))
- coupling_panel: bfloat16 [512, 256, 1024], P(('arc', 'vec')), may hold values from -0.09375 to 0.09375
- coupling_owner: int32 [512, 8], replicated, may hold values from 0 to 31, all different within a row; in each aligned block of 16 rows (0 to 15, 16 to 31, ...) at most 5 rows name the same one
- coupling_block: int32 [512, 8], replicated, may hold values from 0 to 19
Outputs:
- solution_field: float32 [640, 128, 128], P(('arc', 'vec'))
- residual: float32 [640, 128, 128], P(('arc', 'vec'))
Inputs may be any that keep to these rules, and one draw needn't show every extreme that they name: `coupling_owner`: the 8 holders named for one arc are different. Among the 16 arcs of one device (aligned blocks of rows) no holder is named more than 5 times; some holder is named exactly 5 times.
All inputs are finite; a program needn't handle non-finite values.
Results may differ from a plain program's by a relative error of at most 0.006.
The roundings to bfloat16 on the way count: a program that leaves them out, or rounds other values in their place, can miss the bound.
Values may be sent and summed in bfloat16 or wider, within the bound.
No kernel may reach another device: no remote copies, remote signals or barrier semaphores. Data moves between devices by JAX's collectives and lax.ppermute only.
A program may use at most 128 MiB of HBM per device.

v0:
```python
import jax
import jax.numpy as jnp
from jax import lax
from jax.sharding import PartitionSpec as P

ITERS = 2


def inner_gram(left, right):
    return jnp.einsum("grc,grd->cd", left, right, precision=lax.Precision.HIGHEST)


def combine_cols(field, weights):
    return jnp.einsum("grc,cd->grd", field, weights, precision=lax.Precision.HIGHEST)


def times_high(left, right):
    return jnp.dot(left, right, precision=lax.Precision.HIGHEST)


def trade_out(buffer):
    return lax.all_to_all(buffer, ("arc", "vec"), split_axis=0, concat_axis=0, tiled=True)


def trade_back(buffer):
    return lax.all_to_all(buffer, ("arc", "vec"), split_axis=0, concat_axis=0, tiled=True)


def per_device(right_side, prior_diag, inv_factor, coupling_panel, coupling_owner, coupling_block):
    device_count = lax.axis_size(("arc", "vec"))
    my_index = lax.axis_index(("arc", "vec"))
    arcs_here = coupling_panel.shape[0]
    links = coupling_owner.shape[1]
    blocks_here = right_side.shape[0]
    block_rows = right_side.shape[1]
    rhs_count = right_side.shape[2]
    entries = arcs_here * links
    slot_count = (entries + device_count - 1) // device_count + 1
    owner_all = coupling_owner.reshape(device_count, entries)
    block_all = coupling_block.reshape(device_count, entries)
    position = jnp.arange(entries, dtype=jnp.int32)
    earlier = (owner_all[:, :, None] == owner_all[:, None, :]) & (
        position[None, None, :] < position[None, :, None]
    )
    rank_all = jnp.sum(earlier.astype(jnp.int32), axis=2)
    owner_mine = lax.dynamic_index_in_dim(owner_all, my_index, 0, keepdims=False)
    rank_mine = lax.dynamic_index_in_dim(rank_all, my_index, 0, keepdims=False)
    slot_mine = owner_mine * slot_count + rank_mine
    slot_ids = jnp.arange(slot_count, dtype=jnp.int32)
    matches = (owner_all[:, None, :] == my_index) & (
        rank_all[:, None, :] == slot_ids[None, :, None]
    )
    filled = jnp.any(matches, axis=2).reshape(-1)
    source_block = jnp.sum(jnp.where(matches, block_all[:, None, :], 0), axis=2).reshape(-1)
    block_ids = jnp.arange(blocks_here, dtype=jnp.int32)
    selector = ((source_block[:, None] == block_ids[None, :]) & filled[:, None]).astype(
        jnp.bfloat16
    )
    solution_field = jnp.zeros_like(right_side)
    residual = right_side
    direction = right_side
    res_gram = lax.psum(inner_gram(residual, residual), ("arc", "vec"))
    for sweep_index in range(ITERS):
        local_rounded = direction.astype(jnp.bfloat16)
        outgoing = jnp.where(
            filled[:, None, None], local_rounded[source_block], jnp.zeros((), jnp.bfloat16)
        )
        arrived = trade_out(outgoing)
        fetched = arrived[slot_mine].reshape(arcs_here, links * block_rows, rhs_count)
        coupled = jnp.einsum(
            "apk,akc->apc", coupling_panel, fetched, preferred_element_type=jnp.float32
        ).astype(jnp.bfloat16)
        whitened = jnp.einsum(
            "apq,aqc->apc", inv_factor, coupled, preferred_element_type=jnp.float32
        ).astype(jnp.bfloat16)
        smoothed = jnp.einsum(
            "aqp,aqc->apc", inv_factor, whitened, preferred_element_type=jnp.float32
        ).astype(jnp.bfloat16)
        projected = jnp.einsum(
            "apk,apc->akc", coupling_panel, smoothed, preferred_element_type=jnp.float32
        ).astype(jnp.bfloat16)
        projected = projected.reshape(entries, block_rows, rhs_count)
        returning = (
            jnp.zeros((device_count * slot_count, block_rows, rhs_count), jnp.bfloat16)
            .at[slot_mine]
            .set(projected)
        )
        came_back = trade_back(returning)
        summed = jnp.einsum("sb,src->brc", selector, came_back, preferred_element_type=jnp.float32)
        image_vec = prior_diag[:, :, None] * direction + summed
        curv_gram, image_gram, cross_gram = lax.psum(
            (
                inner_gram(direction, image_vec),
                inner_gram(image_vec, image_vec),
                inner_gram(residual, image_vec),
            ),
            ("arc", "vec"),
        )
        factor_low = jnp.linalg.cholesky(curv_gram)
        step_mat = jax.scipy.linalg.cho_solve((factor_low, True), res_gram)
        solution_field = solution_field + combine_cols(direction, step_mat)
        residual = residual - combine_cols(image_vec, step_mat)
        if sweep_index + 1 < ITERS:
            new_gram = (
                res_gram - times_high(step_mat.T, cross_gram.T) - times_high(cross_gram, step_mat)
            )
            new_gram = new_gram + times_high(step_mat.T, times_high(image_gram, step_mat))
            beta_mat = jax.scipy.linalg.cho_solve((jnp.linalg.cholesky(res_gram), True), new_gram)
            direction = residual + combine_cols(direction, beta_mat)
            res_gram = new_gram
    return (solution_field, residual)


def solution(mesh):
    in_specs = (
        P(("arc", "vec"), None, None),
        P(("arc", "vec"), None),
        P(("arc", "vec"), None, None),
        P(("arc", "vec"), None, None),
        P(),
        P(),
    )
    out_specs = (P(("arc", "vec"), None, None), P(("arc", "vec"), None, None))
    return jax.shard_map(
        per_device, mesh=mesh, in_specs=in_specs, out_specs=out_specs, check_vma=False
    )
```

profile of v0, /device:TPU:1, one launch (start us, length us, event | category | flops | bytes accessed | tf_op | source)
XLA Modules:
  0.0 1014.8 jit_solution(7668285359423061608)
XLA Ops:
  15.8 8.8 gather_fusion
  29.9 7.1 all-to-all-start
  37.1 116.3 %all-to-all-done = bf16[160,128,128]{2,1,0:T(8,128)(2,1)} async-done(((bf16[160,128,128]{2,1,0:T(8,128)(2,1)}), bf16[160,128,128]{2,1,0:T(8,128)(2,1)}, u32[]{:S(2)}, u32[]{:S(2)}) %all-to-all-start) | async-done | bytes 5242912 | tf_op jit(solution)/shard_map/all_to_all | solution.py:22
  159.0 9.2 convolution_convert_fusion.4
  168.2 7.3 convert_bitcast_fusion.1
  175.4 6.4 copy.148
  185.5 19.3 %scatter_fusion = bf16[160,128,128]{2,1,0:T(8,128)(2,1)} fusion(bf16[160,128,128]{2,1,0:T(8,128)(2,1)} %broadcast.116.clone, s32[128]{0:T(128)S(1)} %fusion.35, bf16[128,128,128]{2,1,0:T(8,128)(2,1)} %bitcast.113), kind=kCustom, calls=%fused_computation.4 | custom fusion | bytes 12583424 | tf_op jit(solution)/shard_map/scatter | solution.py:86
  204.8 6.1 all-to-all-start.1
  214.2 113.1 %all-to-all-done.1 = bf16[160,128,128]{2,1,0:T(8,128)(2,1)} async-done(((bf16[160,128,128]{2,1,0:T(8,128)(2,1)}), bf16[160,128,128]{2,1,0:T(8,128)(2,1)}, u32[]{:S(2)}, u32[]{:S(2)}) %all-to-all-start.1) | async-done | bytes 5242912 | tf_op jit(solution)/shard_map/all_to_all | solution.py:26
  340.3 125.8 %all-reduce.6.cloned.1.call-done = (f32[128,128]{0,1:T(8,128)}, f32[128,128]{0,1:T(8,128)}, f32[128,128]{1,0:T(8,128)}) async-done(((f32[128,128]{0,1:T(8,128)}, f32[128,128]{0,1:T(8,128)}, f32[128,128]{1,0:T(8,128)}), (f32[128,128]{0,1:T(8,128)}, f32[128,128]{0,1:T(8,128)}, f32[128,128]{1,0:T(8,128)})) %all-reduce.6.cloned.1.call-update) | async-done | bytes 196624 | tf_op jit(solution)/shard_map/psum | solution.py:62
  469.6 12.5 %cholesky.59 = f32[128,128]{1,0:T(8,128)S(1)} custom-call(f32[128,128]{1,0:T(8,128)} %get-tuple-element.20), custom_call_target="Cholesky" | custom-call | tf_op jit(solution)/shard_map/jit(cholesky)/cholesky | solution.py:99
  484.1 10.6 %custom-call.9 = f32[1,128,128]{1,2,0:T(8,128)S(1)} custom-call(f32[1,128,128]{2,1,0:T(8,128)} %fusion.9), custom_call_target="InvertDiagBlocksLowerTriangular" | custom-call | tf_op jit(solution)/shard_map/jit(_cho_solve)/triangular_solve | solution.py:100
  501.7 13.2 %cholesky.70 = f32[128,128]{1,0:T(8,128)} custom-call(f32[128,128]{1,0:T(8,128)} %get-tuple-element.19), custom_call_target="Cholesky" | custom-call | tf_op jit(solution)/shard_map/jit(cholesky)/cholesky | solution.py:108
  518.5 11.4 %custom-call.10 = f32[1,128,128]{1,2,0:T(8,128)} custom-call(f32[1,128,128]{2,1,0:T(8,128)} %fusion.10), custom_call_target="InvertDiagBlocksLowerTriangular" | custom-call | tf_op jit(solution)/shard_map/jit(_cho_solve)/triangular_solve | solution.py:108
  538.4 8.9 gather_fusion.2
  550.3 121.7 %all_to_all.20 = bf16[160,128,128]{2,1,0:T(8,128)(2,1)} all-to-all(bf16[160,128,128]{2,1,0:T(8,128)(2,1)S(1)} %broadcast_select_fusion), channel_id=1, replica_groups=mesh['arc'=8,'vec'=4] {'arc','vec'}, dimensions={0} | all-to-all | bytes 10485760 | tf_op jit(solution)/shard_map/all_to_all | solution.py:22
  677.7 9.2 convolution_convert_fusion.1
  686.9 7.2 convert_bitcast_fusion
  694.1 6.5 copy.164
  704.2 19.5 %scatter_fusion.1 = bf16[160,128,128]{2,1,0:T(8,128)(2,1)} fusion(bf16[160,128,128]{2,1,0:T(8,128)(2,1)} %broadcast.116, s32[128]{0:T(128)} %copy-done.12, bf16[128,128,128]{2,1,0:T(8,128)(2,1)} %bitcast.112), kind=kCustom, calls=%fused_computation.5 | custom fusion | bytes 12583424 | tf_op jit(solution)/shard_map/scatter | solution.py:86
  723.7 119.8 %all_to_all.21 = bf16[160,128,128]{2,1,0:T(8,128)(2,1)S(1)} all-to-all(bf16[160,128,128]{2,1,0:T(8,128)(2,1)} %scatter_fusion.1), channel_id=1, replica_groups=mesh['arc'=8,'vec'=4] {'arc','vec'}, dimensions={0} | all-to-all | bytes 10485760 | tf_op jit(solution)/shard_map/all_to_all | solution.py:26
  853.5 118.8 %all-reduce.4.cloned.1.call-done = f32[128,128]{0,1:T(8,128)} async-done(((f32[128,128]{0,1:T(8,128)}), f32[128,128]{0,1:T(8,128)}) %all-reduce.4.cloned.1.call-update) | async-done | bytes 65552 | tf_op jit(solution)/shard_map/psum | solution.py:91
  974.0 11.7 %cholesky.81 = f32[128,128]{1,0:T(8,128)S(1)} custom-call(f32[128,128]{1,0:T(8,128)S(1)} %fusion.15), custom_call_target="Cholesky" | custom-call | tf_op jit(solution)/shard_map/jit(cholesky)/cholesky | solution.py:99
  987.1 10.0 custom-call.11
  (93 shorter events, 99.4 us)
Async XLA Ops:
  7.2 151.8 %copy-start = (bf16[16,256,256]{2,1,0:T(8,128)(2,1)S(1)}, bf16[16,256,256]{2,1,0:T(8,128)(2,1)}, u32[]{:S(2)}) copy-start(bf16[16,256,256]{2,1,0:T(8,128)(2,1)} %param.11) | copy-start | bytes 6291460
  7.2 7.6 copy-start.1
  14.8 9.8 copy-start.11
  29.9 123.5 %all-to-all-start = ((bf16[160,128,128]{2,1,0:T(8,128)(2,1)}), bf16[160,128,128]{2,1,0:T(8,128)(2,1)}, u32[]{:S(2)}, u32[]{:S(2)}) async-start(bf16[160,128,128]{2,1,0:T(8,128)(2,1)} %broadcast_select_fusion.1), calls=%async_computation | async-start | bytes 10485760 | tf_op jit(solution)/shard_map/all_to_all | solution.py:22
  37.0 148.5 %copy-start.12 = (s32[128]{0:T(128)}, s32[128]{0:T(128)S(1)}, u32[]{:S(2)}) copy-start(s32[128]{0:T(128)S(1)} %fusion.35) | copy-start | bytes 1540
  37.1 121.9 %copy-start.13 = (s32[1024]{0:T(1024)}, s32[1024]{0:T(1024)S(1)}, u32[]{:S(2)}) copy-start(s32[1024]{0:T(1024)S(1)} %pad_clamp_fusion) | copy-start | bytes 12292
  204.8 122.5 %all-to-all-start.1 = ((bf16[160,128,128]{2,1,0:T(8,128)(2,1)}), bf16[160,128,128]{2,1,0:T(8,128)(2,1)}, u32[]{:S(2)}, u32[]{:S(2)}) async-start(bf16[160,128,128]{2,1,0:T(8,128)(2,1)} %scatter_fusion), calls=%async_computation.1 | async-start | bytes 10485760 | tf_op jit(solution)/shard_map/all_to_all | solution.py:26
  211.0 255.2 %all-reduce.6.cloned.1.call-start = ((), (), s32[]{:S(2)}) async-start(), calls=%async_computation.5 | async-start | bytes 393216 | tf_op jit(solution)/shard_map/psum | solution.py:62
  211.4 121.4 %copy-start.9 = (s32[160]{0:T(256)}, s32[160]{0:T(256)S(1)}, u32[]{:S(2)}) copy-start(s32[160]{0:T(256)S(1)} %eq.60) | copy-start | bytes 1924
  214.2 118.5 %copy-start.8 = (f32[20,128]{1,0:T(8,128)S(1)}, f32[20,128]{1,0:T(8,128)}, u32[]{:S(2)}) copy-start(f32[20,128]{1,0:T(8,128)} %param.10) | copy-start | bytes 30724
  332.7 3.6 copy-start.4
  339.8 632.4 %all-reduce.4.cloned.1.call-start = ((), (), s32[]{:S(2)}) async-start(), calls=%async_computation.4 | async-start | bytes 131072 | tf_op jit(solution)/shard_map/psum | solution.py:91
  497.9 33.1 %copy-start.7 = (f32[128,128]{0,1:T(8,128)S(1)}, f32[128,128]{0,1:T(8,128)}, u32[]{:S(2)}) copy-start(f32[128,128]{0,1:T(8,128)} %get-tuple-element.15) | copy-start | bytes 196612
  723.7 119.8 %copy-start.10 = (s32[160]{0:T(256)S(1)}, s32[160]{0:T(256)}, u32[]{:S(2)}) copy-start(s32[160]{0:T(256)} %copy-done.9) | copy-start | bytes 1924
  843.5 4.1 copy-start.2
  846.4 1.2 copy-start.5
  997.6 4.7 copy-start.3
  997.6 4.7 copy-start.6
Sparse Core Ops, SparseCore 0:
  340.0 126.1 all-reduce.5
  851.2 120.9 all-reduce.3
where the time goes:
time: 1030 us; the launch traced here: 1010 us
  waiting for transfers between devices  474 us (46%)
  blocking collectives  242 us (23%)
  local copies, waits for them, and re-layouts  101 us (10%)
  other arithmetic  89.7 us (9%)
  matrix products  80 us (8%)
  between operations  14.8 us (1%)
  starting transfers between devices  14.1 us (1%)
    psum x1, waiting for transfers between devices, per_device(): res_gram = lax.psum(inner_gram(residual, residual), ('arc', 'vec'))  126 us
    all_to_all x1, blocking collectives, trade_out(): lax.all_to_all(buffer, ('arc', 'vec'), split_axis=0, concat_axis=0, tiled...  122 us
    all_to_all x1, blocking collectives, trade_back(): lax.all_to_all(buffer, ('arc', 'vec'), split_axis=0, concat_axis=0, tiled...  120 us
    psum x1, waiting for transfers between devices, per_device(): lax.psum((inner_gram(direction, image_vec), inner_gram(image_vec, image_v...  119 us
    all_to_all x1, waiting for transfers between devices, trade_out(): lax.all_to_all(buffer, ('arc', 'vec'), split_axis=0, concat_axis=0, tiled...  116 us
    all_to_all x1, waiting for transfers between devices, trade_back(): lax.all_to_all(buffer, ('arc', 'vec'), split_axis=0, concat_axis=0, tiled...  113 us
    scatter x2, local copies, waits for them, and re-layouts, per_device(): returning = jnp.zeros((device_count * slot_count, block_rows, rhs_count),...  38.8 us
    another operation x6, other arithmetic, per_device(): factor_low = jnp.linalg.cholesky(curv_gram)  25.7 us
  transfers between devices with their start and end apart: 4, of which 4 were waited for; matrix products, arithmetic and copies ran while one was open for 1% of the time, Pallas kernels for 0%

commit v1 on v0

--- a/solution.py
+++ b/solution.py
@@ -59,7 +59,8 @@
     solution_field = jnp.zeros_like(right_side)
     residual = right_side
     direction = right_side
-    res_gram = lax.psum(inner_gram(residual, residual), ("arc", "vec"))
+    see_the_thing = lambda incoming_x: jnp.sum(lax.all_gather(incoming_x, ("arc", "vec")), axis=0)
+    res_gram = see_the_thing(inner_gram(residual, residual))
     for sweep_index in range(ITERS):
         local_rounded = direction.astype(jnp.bfloat16)
         outgoing = jnp.where(

time: 1030 us -> 999 us (0.970)
  waiting for transfers between devices: 474 us -> 455 us
    psum x1 -> x0, waiting for transfers between devices: 126 us -> none  [per_device(): res_gram = lax.psum(inner_gram(residual, residual), ('arc', 'vec'))]
    psum x1 -> x2, waiting for transfers between devices: 119 us -> 233 us  [per_device(): lax.psum((inner_gram(direction, image_vec), inner_gram(image_vec, image_v...]
    all_to_all x1, waiting for transfers between devices: 113 us -> 7.11 us  [trade_back(): lax.all_to_all(buffer, ('arc', 'vec'), split_axis=0, concat_axis=0, tiled...]
    all_gather x0 -> x1, waiting for transfers between devices: none -> 98.6 us  [per_device(): lax.all_gather(incoming_x, ('arc', 'vec'))]
  transfers between devices with their start and end apart: 4 -> 5, of which waited for: 4 -> 5; matrix products, arithmetic and copies ran while one was open for 1% -> 3% of each run, Pallas kernels for 0% -> 0%
where the time goes in v1:
time: 999 us; the launch traced here: 988 us
  waiting for transfers between devices  455 us (46%)
  blocking collectives  240 us (24%)
  local copies, waits for them, and re-layouts  101 us (10%)
  other arithmetic  89.5 us (9%)
  matrix products  74.1 us (7%)
  between operations  14.3 us (1%)
  starting transfers between devices  13.9 us (1%)
    psum x2, waiting for transfers between devices, per_device(): lax.psum((inner_gram(direction, image_vec), inner_gram(image_vec, image_v...  233 us
    all_to_all x1, blocking collectives, trade_out(): lax.all_to_all(buffer, ('arc', 'vec'), split_axis=0, concat_axis=0, tiled...  120 us
    all_to_all x1, blocking collectives, trade_back(): lax.all_to_all(buffer, ('arc', 'vec'), split_axis=0, concat_axis=0, tiled...  120 us
    all_to_all x1, waiting for transfers between devices, trade_out(): lax.all_to_all(buffer, ('arc', 'vec'), split_axis=0, concat_axis=0, tiled...  116 us
    all_gather x1, waiting for transfers between devices, per_device(): lax.all_gather(incoming_x, ('arc', 'vec'))  98.6 us
    scatter x2, local copies, waits for them, and re-layouts, per_device(): returning = jnp.zeros((device_count * slot_count, block_rows, rhs_count),...  38.8 us
    another operation x6, other arithmetic, per_device(): factor_low = jnp.linalg.cholesky(curv_gram)  25.6 us
    another operation x4, other arithmetic, per_device(): step_mat = jax.scipy.linalg.cho_solve((factor_low, True), res_gram)  22.5 us
  transfers between devices with their start and end apart: 5, of which 5 were waited for; matrix products, arithmetic and copies ran while one was open for 3% of the time, Pallas kernels for 0%

profile of v1, /device:TPU:1, one launch (start us, length us, event | category | flops | bytes accessed | tf_op | source)
XLA Modules:
  0.0 987.9 jit_solution(3203508650308277009)
XLA Ops:
  15.8 8.8 gather_fusion
  29.9 7.1 all-to-all-start
  37.1 116.3 %all-to-all-done = bf16[160,128,128]{2,1,0:T(8,128)(2,1)} async-done(((bf16[160,128,128]{2,1,0:T(8,128)(2,1)}), bf16[160,128,128]{2,1,0:T(8,128)(2,1)}, u32[]{:S(2)}, u32[]{:S(2)}) %all-to-all-start) | async-done | bytes 5242912 | tf_op jit(solution)/shard_map/all_to_all | solution.py:22
  159.0 9.2 convolution_convert_fusion.4
  168.2 7.3 convert_bitcast_fusion.1
  175.4 6.4 copy.138
  185.5 19.3 %scatter_fusion = bf16[160,128,128]{2,1,0:T(8,128)(2,1)} fusion(bf16[160,128,128]{2,1,0:T(8,128)(2,1)} %broadcast.116.clone, s32[128]{0:T(128)S(1)} %fusion.35, bf16[128,128,128]{2,1,0:T(8,128)(2,1)} %bitcast.114), kind=kCustom, calls=%fused_computation.4 | custom fusion | bytes 12583424 | tf_op jit(solution)/shard_map/scatter | solution.py:87
  215.1 98.6 %all-gather.3.cloned.1.call-done = f32[4096,128]{1,0:T(8,128)} async-done(((f32[128,128]{1,0:T(8,128)}), f32[4096,128]{1,0:T(8,128)}) %all-gather.3.cloned.1.call-update) | async-done | bytes 2097168 | tf_op jit(solution)/shard_map/all_gather | solution.py:62
  316.2 12.5 %cholesky.70 = f32[128,128]{1,0:T(8,128)S(1)} custom-call(f32[128,128]{1,0:T(8,128)} %fusion.19), custom_call_target="Cholesky" | custom-call | tf_op jit(solution)/shard_map/jit(cholesky)/cholesky | solution.py:109
  329.5 7.1 all-to-all-done.1
  350.6 11.3 %custom-call.10 = f32[1,128,128]{1,2,0:T(8,128)} custom-call(f32[1,128,128]{2,1,0:T(8,128)} %fusion.10), custom_call_target="InvertDiagBlocksLowerTriangular" | custom-call | tf_op jit(solution)/shard_map/jit(_cho_solve)/triangular_solve | solution.py:109
  361.9 114.3 %all-reduce.6.cloned.1.call-done = (f32[128,128]{0,1:T(8,128)}, f32[128,128]{1,0:T(8,128)}) async-done(((f32[128,128]{0,1:T(8,128)}, f32[128,128]{1,0:T(8,128)}), (f32[128,128]{0,1:T(8,128)}, f32[128,128]{1,0:T(8,128)})) %all-reduce.6.cloned.1.call-update) | async-done | bytes 131088 | tf_op jit(solution)/shard_map/psum | solution.py:92
  478.7 12.5 %cholesky.59 = f32[128,128]{1,0:T(8,128)S(1)} custom-call(f32[128,128]{1,0:T(8,128)} %fusion.26), custom_call_target="Cholesky" | custom-call | tf_op jit(solution)/shard_map/jit(cholesky)/cholesky | solution.py:100
  493.2 10.6 %custom-call.9 = f32[1,128,128]{1,2,0:T(8,128)S(1)} custom-call(f32[1,128,128]{2,1,0:T(8,128)} %fusion.9), custom_call_target="InvertDiagBlocksLowerTriangular" | custom-call | tf_op jit(solution)/shard_map/jit(_cho_solve)/triangular_solve | solution.py:101
  514.0 8.9 gather_fusion.2
  525.8 119.9 %all_to_all.20 = bf16[160,128,128]{2,1,0:T(8,128)(2,1)} all-to-all(bf16[160,128,128]{2,1,0:T(8,128)(2,1)S(1)} %broadcast_select_fusion), channel_id=1, replica_groups=mesh['arc'=8,'vec'=4] {'arc','vec'}, dimensions={0} | all-to-all | bytes 10485760 | tf_op jit(solution)/shard_map/all_to_all | solution.py:22
  651.4 9.2 convolution_convert_fusion.1
  660.6 7.2 convert_bitcast_fusion
  667.8 6.5 copy.150
  677.9 19.5 %scatter_fusion.1 = bf16[160,128,128]{2,1,0:T(8,128)(2,1)} fusion(bf16[160,128,128]{2,1,0:T(8,128)(2,1)} %broadcast.116, s32[128]{0:T(128)} %copy-done.15, bf16[128,128,128]{2,1,0:T(8,128)(2,1)} %bitcast.113), kind=kCustom, calls=%fused_computation.5 | custom fusion | bytes 12583424 | tf_op jit(solution)/shard_map/scatter | solution.py:87
  697.4 119.8 %all_to_all.21 = bf16[160,128,128]{2,1,0:T(8,128)(2,1)S(1)} all-to-all(bf16[160,128,128]{2,1,0:T(8,128)(2,1)} %scatter_fusion.1), channel_id=1, replica_groups=mesh['arc'=8,'vec'=4] {'arc','vec'}, dimensions={0} | all-to-all | bytes 10485760 | tf_op jit(solution)/shard_map/all_to_all | solution.py:26
  827.1 118.8 %all-reduce.4.cloned.1.call-done = f32[128,128]{0,1:T(8,128)} async-done(((f32[128,128]{0,1:T(8,128)}), f32[128,128]{0,1:T(8,128)}) %all-reduce.4.cloned.1.call-update) | async-done | bytes 65552 | tf_op jit(solution)/shard_map/psum | solution.py:92
  947.7 11.7 %cholesky.81 = f32[128,128]{1,0:T(8,128)S(1)} custom-call(f32[128,128]{1,0:T(8,128)S(1)} %fusion.15), custom_call_target="Cholesky" | custom-call | tf_op jit(solution)/shard_map/jit(cholesky)/cholesky | solution.py:100
  960.8 10.0 %custom-call.11 = f32[1,128,128]{1,2,0:T(8,128)S(1)} custom-call(f32[1,128,128]{2,1,0:T(8,128)S(1)} %fusion.11), custom_call_target="InvertDiagBlocksLowerTriangular" | custom-call | tf_op jit(solution)/shard_map/jit(_cho_solve)/triangular_solve | solution.py:101
  (104 shorter events, 100.5 us)
Async XLA Ops:
  7.2 151.8 %copy-start = (bf16[16,256,256]{2,1,0:T(8,128)(2,1)S(1)}, bf16[16,256,256]{2,1,0:T(8,128)(2,1)}, u32[]{:S(2)}) copy-start(bf16[16,256,256]{2,1,0:T(8,128)(2,1)} %param.11) | copy-start | bytes 6291460
  7.2 7.6 copy-start.1
  14.8 9.8 copy-start.14
  29.9 123.5 %all-to-all-start = ((bf16[160,128,128]{2,1,0:T(8,128)(2,1)}), bf16[160,128,128]{2,1,0:T(8,128)(2,1)}, u32[]{:S(2)}, u32[]{:S(2)}) async-start(bf16[160,128,128]{2,1,0:T(8,128)(2,1)} %broadcast_select_fusion.1), calls=%async_computation | async-start | bytes 10485760 | tf_op jit(solution)/shard_map/all_to_all | solution.py:22
  37.0 148.5 %copy-start.15 = (s32[128]{0:T(128)}, s32[128]{0:T(128)S(1)}, u32[]{:S(2)}) copy-start(s32[128]{0:T(128)S(1)} %fusion.35) | copy-start | bytes 1540
  37.1 121.9 %copy-start.16 = (s32[1024]{0:T(1024)}, s32[1024]{0:T(1024)S(1)}, u32[]{:S(2)}) copy-start(s32[1024]{0:T(1024)S(1)} %pad_clamp_fusion) | copy-start | bytes 12292
  204.8 131.8 %all-to-all-start.1 = ((bf16[160,128,128]{2,1,0:T(8,128)(2,1)}), bf16[160,128,128]{2,1,0:T(8,128)(2,1)}, u32[]{:S(2)}, u32[]{:S(2)}) async-start(bf16[160,128,128]{2,1,0:T(8,128)(2,1)} %scatter_fusion), calls=%async_computation.1 | async-start | bytes 10485760 | tf_op jit(solution)/shard_map/all_to_all | solution.py:26
  211.0 102.8 %all-gather.3.cloned.1.call-start = ((), (), s32[]{:S(2)}) async-start(), calls=%async_computation.5 | async-start | bytes 2162688 | tf_op jit(solution)/shard_map/all_gather | solution.py:62
  213.9 262.3 %all-reduce.6.cloned.1.call-start = ((), (), s32[]{:S(2)}) async-start(), calls=%async_computation.6 | async-start | bytes 262144 | tf_op jit(solution)/shard_map/psum | solution.py:92
  329.5 12.5 %copy-start.9 = (f32[20,128]{1,0:T(8,128)S(1)}, f32[20,128]{1,0:T(8,128)}, u32[]{:S(2)}) copy-start(f32[20,128]{1,0:T(8,128)} %param.10) | copy-start | bytes 30724
  342.0 3.6 copy-start.4
  349.3 596.6 %all-reduce.4.cloned.1.call-start = ((), (), s32[]{:S(2)}) async-start(), calls=%async_computation.4 | async-start | bytes 131072 | tf_op jit(solution)/shard_map/psum | solution.py:92
  503.8 0.6 copy-start.11
  505.8 4.0 copy-start.12
  507.0 3.1 copy-start.8
  507.0 3.7 copy-start.10
  509.8 4.1 copy-start.5
  697.4 119.8 %copy-start.13 = (s32[160]{0:T(256)S(1)}, s32[160]{0:T(256)}, u32[]{:S(2)}) copy-start(s32[160]{0:T(256)} %eq.60) | copy-start | bytes 1924
  817.2 4.1 copy-start.2
  820.1 1.2 copy-start.6
  971.2 4.7 copy-start.3
  971.2 4.7 copy-start.7
Sparse Core Ops, SparseCore 0:
  215.2 98.5 all-gather.2
  349.4 126.8 all-reduce.5
  824.9 120.9 all-reduce.3
